TPU v7x, 256 devices: a whole 4x4x8 slice. The times are simulated.
256 devices in a mesh: wide: 32 (over y, x, core), narrow: 8 (over z).
Axes of the slice: x: 4, y: 4, z: 8, core: 2. Of those that a mesh axis runs over, the one named last changes fastest.
Arguments:
- amplitudes: bfloat16 [1024, 16, 4096], P('wide', None, 'narrow'), may hold values from -6 to 6
- amp_tiles: int32 [32, 16], replicated, may hold values from 0 to 31, all different within a row
- integrals: bfloat16 [32, 2, 4096, 4096], P('wide', None, None, 'narrow'), may hold values from -0.09375 to 0.09375
- cd_tiles: int32 [32, 2], replicated, may hold values from 0 to 31, all different within a row
- q_owner: int32 [32], replicated, may hold values from 0 to 31, each once
Outputs:
- residual: bfloat16 [1024, 32, 4096], P('wide', None, 'narrow')
Inputs may be any that keep to these rules, and one draw needn't show every extreme that they name: `amp_tiles`: within a row, the 16 tiles are different. `cd_tiles`: within a row, the 2 tiles are different; every tile is named by some row. `q_owner`: each owner index appears once.
All inputs are finite; a program needn't handle non-finite values.
Results may differ from a plain program's by a relative error of at most 0.017.
Values may be sent and summed in bfloat16 or wider, within the bound.
A program may use at most 64 MiB of HBM per device.

v0:
```python
import jax
import jax.numpy as jnp
from jax import lax
from jax.sharding import PartitionSpec as P


def on_device(amplitudes, amp_tiles, integrals, cd_tiles, q_owner):
    my_index = lax.axis_index("wide")
    blocks = lax.axis_size("wide")
    rows_dev = amplitudes.shape[0]
    local_ints = integrals[0]
    tile_ids = jnp.arange(q_owner.shape[0], dtype=jnp.int32)
    holder = (q_owner[None, :] == jnp.arange(blocks, dtype=jnp.int32)[:, None]).astype(jnp.int32)
    owned_tile = jnp.sum(holder * tile_ids[None, :], axis=1)
    wanted = cd_tiles[owned_tile]
    my_wanted = wanted[my_index]
    segment = lax.all_gather(amplitudes, "wide", axis=0, tiled=True)
    length = segment.shape[0]
    source = jnp.arange(length, dtype=jnp.int32) // rows_dev
    tile_list = amp_tiles[source]
    picker = (tile_list[:, :, None] == my_wanted[None, None, :]).astype(jnp.bfloat16)
    chosen = jnp.einsum("rtk,rtc->rkc", picker, segment, preferred_element_type=jnp.float32).astype(
        jnp.bfloat16
    )
    partial_value = jnp.einsum(
        "rkc,kpc->rp", chosen, local_ints, preferred_element_type=jnp.float32
    )
    shares = lax.psum_scatter(
        partial_value.astype(jnp.bfloat16), "narrow", scatter_dimension=1, tiled=True
    )
    returned = lax.all_to_all(
        shares.reshape(blocks, rows_dev, shares.shape[1]),
        "wide",
        split_axis=0,
        concat_axis=0,
        tiled=True,
    )
    result = jnp.take(returned, q_owner, axis=0)
    return jnp.transpose(result, (1, 0, 2))


def solution(mesh):
    placed = (P("wide", None, "narrow"), P(), P("wide", None, None, "narrow"), P(), P())
    return jax.shard_map(
        on_device, mesh=mesh, in_specs=placed, out_specs=P("wide", None, "narrow"), check_vma=False
    )
```

profile of v0, /device:TPU:1, one launch (start us, length us, event | category | flops | bytes accessed | tf_op | source)
XLA Modules:
  0.0 242.8 jit_solution(6019152147181182622)
XLA Ops:
  6.5 0.0 all-gather.2.cloned.1.call-start
  6.5 0.7 all-gather.2.cloned.1.call-update
  7.3 0.0 reduce-scatter.2.cloned.1.call-start
  7.3 0.8 copy.16
  8.1 0.8 copy.15
  8.8 0.8 select_reduce_fusion
  9.6 0.6 gather_fusion.1
  10.2 2.8 %gather_fusion = s32[1024,16]{1,0:T(8,128)S(1)} fusion(s32[32,16]{1,0:T(8,128)S(1)} %copy.15, s32[1024]{0:T(1024)S(1)} %broadcast_clamp_fusion), kind=kCustom, calls=%fused_computation | custom fusion | bytes 135168 | tf_op jit(solution)/shard_map/gather | solution.py:20
  13.1 78.6 %all-gather.2.cloned.1.call-done = bf16[1024,16,512]{2,1,0:T(8,128)(2,1)} async-done(((bf16[32,16,512]{2,1,0:T(8,128)(2,1)}), bf16[1024,16,512]{2,1,0:T(8,128)(2,1)}) %all-gather.2.cloned.1.call-update) | async-done | bytes 16777232 | tf_op jit(solution)/shard_map/all_gather | solution.py:17
  91.7 8.6 %convolution_convert_fusion = bf16[1024,2,512]{2,1,0:T(2,128)(2,1)S(1)} fusion(bf16[1024,16,512]{2,1,0:T(8,128)(2,1)} %all-gather.2.cloned.1.call-done, s32[1024,16]{1,0:T(8,128)S(1)} %gather_fusion, s32[2]{0:T(128)S(1)} %dynamic-slice_bitcast_fusion), kind=kOutput, calls=%fused_computation.5 | convolution fusion | flops 34635776 | bytes 18939912 | tf_op jit(solution)/shard_map/rtk,rtc->rkc/dot_general | solution.py:22
  100.3 14.4 %bitcast_convert_fusion = bf16[1024,4096]{1,0:T(8,128)(2,1)} fusion(bf16[1,2,4096,512]{3,2,1,0:T(8,128)(2,1)} %param.7, bf16[1024,2,512]{2,1,0:T(2,128)(2,1)S(1)} %convolution_convert_fusion), kind=kOutput, calls=%fused_computation.3 | convolution fusion | flops 8594128896 | bytes 18874368 | tf_op jit(solution)/shard_map/rkc,kpc->rp/dot_general | solution.py:25
  114.6 0.0 copy-start
  114.7 0.0 reduce-scatter.2.cloned.1.call-update
  114.7 94.2 %reduce-scatter.2.cloned.1.call-done = bf16[1024,512]{1,0:T(8,128)(2,1)} async-done(((bf16[1024,4096]{1,0:T(8,128)(2,1)}), bf16[1024,512]{1,0:T(8,128)(2,1)}) %reduce-scatter.2.cloned.1.call-update) | async-done | bytes 1048592 | tf_op jit(solution)/shard_map/reduce_scatter | solution.py:28
  208.9 7.5 %all-to-all-start = ((bf16[32,32,512]{2,1,0:T(8,128)(2,1)}), bf16[32,32,512]{2,1,0:T(8,128)(2,1)S(1)}, u32[]{:S(2)}, u32[]{:S(2)}) async-start(bf16[32,32,512]{2,1,0:T(8,128)(2,1)} %bitcast.16), calls=%async_computation.1 | async-start | bytes 2097152 | tf_op jit(solution)/shard_map/all_to_all | solution.py:31
  216.4 0.0 copy-done
  216.5 17.1 %all-to-all-done = bf16[32,32,512]{2,1,0:T(8,128)(2,1)S(1)} async-done(((bf16[32,32,512]{2,1,0:T(8,128)(2,1)}), bf16[32,32,512]{2,1,0:T(8,128)(2,1)S(1)}, u32[]{:S(2)}, u32[]{:S(2)}) %all-to-all-start) | async-done | bytes 1048608 | tf_op jit(solution)/shard_map/all_to_all | solution.py:31
  233.6 0.6 gather_fusion.2
  234.2 0.2 select_bitcast_fusion
  234.4 1.5 copy.18
  (8 shorter events, 0.1 us)
Async XLA Ops:
  6.5 85.1 %all-gather.2.cloned.1.call-start = ((), (), s32[]{:S(2)}) async-start(), calls=%async_computation.2 | async-start | bytes 17301504 | tf_op jit(solution)/shard_map/all_gather | solution.py:17
  7.3 201.7 %reduce-scatter.2.cloned.1.call-start = ((), (), s32[]{:S(2)}) async-start(), calls=%async_computation.3 | async-start | bytes 9437184 | tf_op jit(solution)/shard_map/reduce_scatter | solution.py:28
  114.6 101.8 %copy-start = (s32[32]{0:T(128)S(1)}, s32[32]{0:T(128)}, u32[]{:S(2)}) copy-start(s32[32]{0:T(128)} %param.9) | copy-start | bytes 388
  208.9 24.7 %all-to-all-start = ((bf16[32,32,512]{2,1,0:T(8,128)(2,1)}), bf16[32,32,512]{2,1,0:T(8,128)(2,1)S(1)}, u32[]{:S(2)}, u32[]{:S(2)}) async-start(bf16[32,32,512]{2,1,0:T(8,128)(2,1)} %bitcast.16), calls=%async_computation.1 | async-start | bytes 2097152 | tf_op jit(solution)/shard_map/all_to_all | solution.py:31
Sparse Core Ops, SparseCore 0:
  9.9 81.7 all-gather.1
  114.8 94.0 reduce-scatter.1
where the time goes:
time: 243 us
  waiting for transfers between devices  191 us (79%)
  matrix products  23 us (9%)
  between operations  13.5 us (6%)
  starting transfers between devices  7.52 us (3%)
  local copies, waits for them, and re-layouts  7.09 us (3%)
    reduce_scatter x1, waiting for transfers between devices, on_device(): lax.psum_scatter(partial_value.astype(jnp.bfloat16), 'narrow', scatter_di...  94.2 us
    all_gather x1, waiting for transfers between devices, on_device(): segment = lax.all_gather(amplitudes, 'wide', axis=0, tiled=True)  78.6 us
    all_to_all x1, waiting for transfers between devices, on_device(): lax.all_to_all(shares.reshape(blocks, rows_dev, shares.shape[1]), 'wide',...  17.1 us
    dot_general x1, matrix products, on_device(): jnp.einsum('rkc,kpc->rp', chosen, local_ints, preferred_element_type=jnp....  14.4 us
    dot_general x1, matrix products, on_device(): jnp.einsum('rtk,rtc->rkc', picker, segment, preferred_element_type=jnp.fl...  8.62 us
    all_to_all x1, starting transfers between devices, on_device(): lax.all_to_all(shares.reshape(blocks, rows_dev, shares.shape[1]), 'wide',...  7.48 us
  transfers between devices with their start and end apart: 3, of which 3 were waited for; matrix products, arithmetic and copies ran while one was open for 2% of the time, Pallas kernels for 0%

commit v1 on v0

--- a/solution.py
+++ b/solution.py
@@ -2,6 +2,11 @@
 import jax.numpy as jnp
 from jax import lax
 from jax.sharding import PartitionSpec as P
+
+
+def gather_by_exchange(x, axis, dim):
+    copies = jnp.concatenate([x] * lax.axis_size(axis), axis=dim)
+    return lax.all_to_all(copies, axis, dim, dim, tiled=True)
 
 
 def on_device(amplitudes, amp_tiles, integrals, cd_tiles, q_owner):
@@ -14,7 +19,7 @@
     owned_tile = jnp.sum(holder * tile_ids[None, :], axis=1)
     wanted = cd_tiles[owned_tile]
     my_wanted = wanted[my_index]
-    segment = lax.all_gather(amplitudes, "wide", axis=0, tiled=True)
+    segment = gather_by_exchange(amplitudes, "wide", 0)
     length = segment.shape[0]
     source = jnp.arange(length, dtype=jnp.int32) // rows_dev
     tile_list = amp_tiles[source]

time: 243 us -> 423 us (1.74)
  waiting for transfers between devices: 191 us -> 319 us
  local copies, waits for them, and re-layouts: 7.09 us -> 50.4 us
  starting transfers between devices: 7.52 us -> 16.3 us
    all_to_all x0 -> x1, waiting for transfers between devices: none -> 197 us  [gather_by_exchange(): return lax.all_to_all(copies, axis, dim, dim, tiled=True)]
    all_gather x1 -> x0, waiting for transfers between devices: 78.6 us -> none  [on_device(): segment = lax.all_gather(amplitudes, 'wide', axis=0, tiled=True)]
    unnamed x4 -> x41, local copies, waits for them, and re-layouts: 1.53 us -> 42.9 us
    reduce_scatter x1, waiting for transfers between devices: 94.2 us -> 104 us  [on_device(): lax.psum_scatter(partial_value.astype(jnp.bfloat16), 'narrow', scatter_di...]
    all_to_all x0 -> x1, starting transfers between devices: none -> 8.77 us  [gather_by_exchange(): return lax.all_to_all(copies, axis, dim, dim, tiled=True)]
  transfers between devices with their start and end apart: 3 -> 3, of which waited for: 3 -> 3; matrix products, arithmetic and copies ran while one was open for 2% -> 1% of each run, Pallas kernels for 0% -> 0%
where the time goes in v1:
time: 423 us; the launch traced here: 422 us
  waiting for transfers between devices  319 us (75%)
  local copies, waits for them, and re-layouts  50.4 us (12%)
  matrix products  23 us (5%)
  starting transfers between devices  16.3 us (4%)
  between operations  13.5 us (3%)
    all_to_all x1, waiting for transfers between devices, gather_by_exchange(): return lax.all_to_all(copies, axis, dim, dim, tiled=True)  197 us
    reduce_scatter x1, waiting for transfers between devices, on_device(): lax.psum_scatter(partial_value.astype(jnp.bfloat16), 'narrow', scatter_di...  104 us
    unnamed x41, local copies, waits for them, and re-layouts  42.9 us
    all_to_all x1, waiting for transfers between devices, on_device(): lax.all_to_all(shares.reshape(blocks, rows_dev, shares.shape[1]), 'wide',...  17.1 us
    dot_general x1, matrix products, on_device(): jnp.einsum('rkc,kpc->rp', chosen, local_ints, preferred_element_type=jnp....  14.4 us
    all_to_all x1, starting transfers between devices, gather_by_exchange(): return lax.all_to_all(copies, axis, dim, dim, tiled=True)  8.77 us
    dot_general x1, matrix products, on_device(): jnp.einsum('rtk,rtc->rkc', picker, segment, preferred_element_type=jnp.fl...  8.64 us
  transfers between devices with their start and end apart: 3, of which 3 were waited for; matrix products, arithmetic and copies ran while one was open for 1% of the time, Pallas kernels for 0%

profile of v1, /device:TPU:1, one launch (start us, length us, event | category | flops | bytes accessed | tf_op | source)
XLA Modules:
  0.0 422.2 jit_solution(11341409414122779540)
XLA Ops:
  6.5 1.9 constant_dynamic-update-slice_fusion.31
  8.5 1.9 constant_dynamic-update-slice_fusion.30
  10.3 1.9 constant_dynamic-update-slice_fusion.29
  12.2 1.9 constant_dynamic-update-slice_fusion.28
  14.1 1.9 constant_dynamic-update-slice_fusion.27
  16.0 1.9 constant_dynamic-update-slice_fusion.26
  17.9 1.9 constant_dynamic-update-slice_fusion.25
  19.7 1.9 constant_dynamic-update-slice_fusion.24
  21.6 1.9 constant_dynamic-update-slice_fusion.23
  23.5 1.9 constant_dynamic-update-slice_fusion.22
  25.3 1.9 constant_dynamic-update-slice_fusion.21
  27.2 1.9 constant_dynamic-update-slice_fusion.20
  29.1 1.9 constant_dynamic-update-slice_fusion.19
  31.0 1.9 constant_dynamic-update-slice_fusion.18
  32.9 1.8 constant_dynamic-update-slice_fusion.17
  34.7 1.9 constant_dynamic-update-slice_fusion.16
  36.6 0.9 constant_dynamic-update-slice_fusion.15
  37.5 0.9 constant_dynamic-update-slice_fusion.14
  40.0 0.9 constant_dynamic-update-slice_fusion.11
  42.5 0.8 constant_dynamic-update-slice_fusion.8
  46.7 0.9 constant_dynamic-update-slice_fusion.3
  47.6 0.9 constant_dynamic-update-slice_fusion.2
  50.1 8.8 %all-to-all-start = ((bf16[1024,16,512]{2,1,0:T(8,128)(2,1)}), bf16[1024,16,512]{2,1,0:T(8,128)(2,1)}, u32[]{:S(2)}, u32[]{:S(2)}) async-start(bf16[1024,16,512]{2,1,0:T(8,128)(2,1)} %constant_dynamic-update-slice_fusion), calls=%async_computation | async-start | bytes 33554432 | tf_op jit(solution)/shard_map/all_to_all | solution.py:9
  59.3 2.8 gather_fusion
  63.0 0.9 copy.14
  63.9 196.9 %all-to-all-done = bf16[1024,16,512]{2,1,0:T(8,128)(2,1)} async-done(((bf16[1024,16,512]{2,1,0:T(8,128)(2,1)}), bf16[1024,16,512]{2,1,0:T(8,128)(2,1)}, u32[]{:S(2)}, u32[]{:S(2)}) %all-to-all-start) | async-done | bytes 16777248 | tf_op jit(solution)/shard_map/all_to_all | solution.py:9
  260.8 8.6 %convolution_convert_fusion = bf16[1024,2,512]{2,1,0:T(2,128)(2,1)S(1)} fusion(pred[1024,16,2]{1,2,0:T(4,128)(4,1)S(1)} %copy.14, bf16[1024,16,512]{2,1,0:T(8,128)(2,1)} %all-to-all-done), kind=kOutput, calls=%fused_computation.5 | convolution fusion | flops 34603008 | bytes 18907136 | tf_op jit(solution)/shard_map/rtk,rtc->rkc/dot_general | solution.py:27
  269.5 14.4 %bitcast_convert_fusion = bf16[1024,4096]{1,0:T(8,128)(2,1)} fusion(bf16[1,2,4096,512]{3,2,1,0:T(8,128)(2,1)} %param.7, bf16[1024,2,512]{2,1,0:T(2,128)(2,1)S(1)} %convolution_convert_fusion), kind=kOutput, calls=%fused_computation.3 | convolution fusion | flops 8594128896 | bytes 18874368 | tf_op jit(solution)/shard_map/rkc,kpc->rp/dot_general | solution.py:30
  283.9 104.5 %reduce-scatter.2.cloned.1.call-done = bf16[1024,512]{1,0:T(8,128)(2,1)} async-done(((bf16[1024,4096]{1,0:T(8,128)(2,1)}), bf16[1024,512]{1,0:T(8,128)(2,1)}) %reduce-scatter.2.cloned.1.call-update) | async-done | bytes 1048592 | tf_op jit(solution)/shard_map/reduce_scatter | solution.py:33
  388.3 7.5 %all-to-all-start.1 = ((bf16[32,32,512]{2,1,0:T(8,128)(2,1)}), bf16[32,32,512]{2,1,0:T(8,128)(2,1)S(1)}, u32[]{:S(2)}, u32[]{:S(2)}) async-start(bf16[32,32,512]{2,1,0:T(8,128)(2,1)} %bitcast.17), calls=%async_computation.2 | async-start | bytes 2097152 | tf_op jit(solution)/shard_map/all_to_all | solution.py:36
  395.9 17.1 %all-to-all-done.1 = bf16[32,32,512]{2,1,0:T(8,128)(2,1)S(1)} async-done(((bf16[32,32,512]{2,1,0:T(8,128)(2,1)}), bf16[32,32,512]{2,1,0:T(8,128)(2,1)S(1)}, u32[]{:S(2)}, u32[]{:S(2)}) %all-to-all-start.1) | async-done | bytes 1048608 | tf_op jit(solution)/shard_map/all_to_all | solution.py:36
  413.8 1.5 copy.16
  (35 shorter events, 10.3 us)
Async XLA Ops:
  6.5 30.1 %copy-start = (bf16[32,16,512]{2,1,0:T(8,128)(2,1)S(1)}, bf16[32,16,512]{2,1,0:T(8,128)(2,1)}, u32[]{:S(2)}) copy-start(bf16[32,16,512]{2,1,0:T(8,128)(2,1)} %param.5) | copy-start | bytes 1572868
  50.1 8.8 %copy-start.2 = (s32[32,2]{0,1:T(2,128)S(1)}, s32[32,2]{0,1:T(2,128)}, u32[]{:S(2)}) copy-start(s32[32,2]{0,1:T(2,128)} %param.8) | copy-start | bytes 772
  50.1 8.9 %copy-start.1 = (s32[32,16]{0,1:T(8,128)S(1)}, s32[32,16]{0,1:T(8,128)}, u32[]{:S(2)}) copy-start(s32[32,16]{0,1:T(8,128)} %param.6) | copy-start | bytes 6148
  50.1 9.0 %copy-start.3 = (s32[32]{0:T(128)S(1)}, s32[32]{0:T(128)}, u32[]{:S(2)}) copy-start(s32[32]{0:T(128)} %param.9) | copy-start | bytes 388
  50.1 210.7 %all-to-all-start = ((bf16[1024,16,512]{2,1,0:T(8,128)(2,1)}), bf16[1024,16,512]{2,1,0:T(8,128)(2,1)}, u32[]{:S(2)}, u32[]{:S(2)}) async-start(bf16[1024,16,512]{2,1,0:T(8,128)(2,1)} %constant_dynamic-update-slice_fusion), calls=%async_computation | async-start | bytes 33554432 | tf_op jit(solution)/shard_map/all_to_all | solution.py:9
  58.9 329.5 %reduce-scatter.2.cloned.1.call-start = ((), (), s32[]{:S(2)}) async-start(), calls=%async_computation.3 | async-start | bytes 9437184 | tf_op jit(solution)/shard_map/reduce_scatter | solution.py:33
  388.3 24.7 %all-to-all-start.1 = ((bf16[32,32,512]{2,1,0:T(8,128)(2,1)}), bf16[32,32,512]{2,1,0:T(8,128)(2,1)S(1)}, u32[]{:S(2)}, u32[]{:S(2)}) async-start(bf16[32,32,512]{2,1,0:T(8,128)(2,1)} %bitcast.17), calls=%async_computation.2 | async-start | bytes 2097152 | tf_op jit(solution)/shard_map/all_to_all | solution.py:36
Sparse Core Ops, SparseCore 0:
  284.0 104.3 reduce-scatter.1
